TPU v7x, 128 devices: a whole 4x4x4 slice. The times are simulated.
128 devices in a mesh: lsec: 8 (over y, core), rsec: 16 (over x, z).
Axes of the slice: x: 4, y: 4, z: 4, core: 2. Of those that a mesh axis runs over, the one named last changes fastest.
Arguments:
- two_site: bfloat16 [2, 32, 128, 8192], P(None, 'lsec', None, 'rsec'), may hold values from -6 to 6
- left_env: bfloat16 [34, 32, 128, 128], P(None, 'lsec', 'rsec'), may hold values from -0.09375 to 0.09375
- right_env: bfloat16 [34, 64, 128, 128], P(None, 'rsec', 'lsec'), may hold values from -0.5 to 0.5
- left_size: int32 [32], P('lsec'), may hold values from 16 to 128, as said below
- right_size: int32 [64], P('rsec'), may hold values from 16 to 128, as said below
- channel_shift: int32 [34, 2], replicated, may hold values from -2 to 2, as said below
Outputs:
- applied: bfloat16 [2, 32, 128, 8192], P(None, 'lsec', None, 'rsec')
Inputs may be any that keep to these rules, and one draw needn't show every extreme that they name: `left_size`: each sector holds 16 to 128 states; some left sector and some right sector hold exactly 128. `right_size`: as for left_size. `channel_shift`: every offset from -2 to 2 is the left offset of some channel and the right offset of some channel.
All inputs are finite; a program needn't handle non-finite values.
Results may differ from a plain program's by a relative error of at most 0.0049.
Values may be sent and summed in bfloat16 or wider, within the bound.
No kernel may reach another device: no remote copies, remote signals or barrier semaphores. Data moves between devices by JAX's collectives and lax.ppermute only.
A program may use at most 64 MiB of HBM per device.

v0:
```python
import functools

import jax
import jax.numpy as jnp
from jax import lax
from jax.experimental import pallas as pl
from jax.experimental.pallas import tpu as pltpu
from jax.sharding import PartitionSpec as P


KCH = 34
SHIFT = 2
SPLIT = 16
STAGED = 4
XN, ZN, YN, CORES = 4, 4, 4, 2
NT = (((1,), (1,)), ((), ()))
NN = (((1,), (0,)), ((), ()))


def shifted_x(step):
    return [(ZN * x + z, ZN * ((x + step) % XN) + z) for x in range(XN) for z in range(ZN)]


def shifted_z(step):
    return [(ZN * x + z, ZN * x + (z + step) % ZN) for x in range(XN) for z in range(ZN)]


def shifted_y(step):
    return [(CORES * y + c, CORES * ((y + step) % YN) + c) for y in range(YN) for c in range(CORES)]


def prepare_kernel(
    left_size, right_size, two_site, left_env, first, second, down, up,
    rows_live, cols_live, held, env, sems,
):
    pairs = ((left_env, env), (left_size, rows_live), (right_size, cols_live), (two_site, held))
    copies = [
        pltpu.make_async_copy(src, dst, sems.at[at]) for at, (src, dst) in enumerate(pairs)
    ]
    for copy in copies:
        copy.start()
    copies[0].wait()
    first[...] = env[:SPLIT]
    second[...] = env[SPLIT:]
    for copy in copies[1:]:
        copy.wait()
    row = lax.broadcasted_iota(jnp.int32, (128, 128), 0)
    col = lax.broadcasted_iota(jnp.int32, (128, 128), 1)
    for l in range(4):
        for r in range(4):
            live = (row < rows_live[l]) & (col < cols_live[r])
            target = down if r < 2 else up
            for v in range(2):
                block = held[v, l, :, r * 128 : r * 128 + 128].astype(jnp.float32)
                target[r % 2, l, v * 128 : v * 128 + 128] = jnp.where(live, block, 0.0).astype(
                    jnp.bfloat16
                )


def prepared(two_site, left_env, left_size, right_size):
    half = jax.ShapeDtypeStruct((2, 4, 256, 128), jnp.bfloat16)
    parts = [
        jax.ShapeDtypeStruct((many, 4, 8, 128), jnp.bfloat16) for many in (SPLIT, KCH - SPLIT)
    ]
    return pl.pallas_call(
        prepare_kernel,
        out_shape=(*parts, half, half),
        in_specs=[pl.BlockSpec(memory_space=pltpu.HBM)] * 4,
        out_specs=(pl.BlockSpec(memory_space=pltpu.VMEM),) * 4,
        scratch_shapes=[
            pltpu.SMEM((4,), jnp.int32),
            pltpu.SMEM((4,), jnp.int32),
            pltpu.VMEM(two_site.shape, jnp.bfloat16),
            pltpu.VMEM(left_env.shape, jnp.bfloat16),
            pltpu.SemaphoreType.DMA((4,)),
        ],
        compiler_params=pltpu.CompilerParams(vmem_limit_bytes=60 * 1024 * 1024),
        cost_estimate=pl.CostEstimate(flops=1 << 20, bytes_accessed=2 << 20, transcendentals=0),
    )(left_size, right_size, two_site, left_env)


def rim_kernel(low_r, down, up, high_r, to_next, to_previous):
    for at, part in enumerate((low_r, down, up, high_r)):
        to_next[2 * at : 2 * at + 2] = part[:, 2:4]
        to_previous[2 * at : 2 * at + 2] = part[:, 0:2]


def left_rims(low_r, down, up, high_r):
    rim = jax.ShapeDtypeStruct((8, 2, 256, 128), jnp.bfloat16)
    vmem = pl.BlockSpec(memory_space=pltpu.VMEM)
    return pl.pallas_call(
        rim_kernel,
        out_shape=(rim, rim),
        in_specs=[vmem] * 4,
        out_specs=(vmem, vmem),
        compiler_params=pltpu.CompilerParams(vmem_limit_bytes=12 << 20),
        cost_estimate=pl.CostEstimate(flops=1 << 20, bytes_accessed=4 << 20, transcendentals=0),
    )(low_r, down, up, high_r)


def bundle_kernel(own, left, right, far, out):
    for at, part in enumerate((own, left, right, far)):
        out[at] = part[...]


def bundled(own, left, right, far):
    vmem = pl.BlockSpec(memory_space=pltpu.VMEM)
    return pl.pallas_call(
        bundle_kernel,
        out_shape=jax.ShapeDtypeStruct((4, *own.shape), jnp.bfloat16),
        in_specs=[vmem] * 4,
        out_specs=vmem,
        compiler_params=pltpu.CompilerParams(vmem_limit_bytes=8 << 20),
        cost_estimate=pl.CostEstimate(flops=1 << 20, bytes_accessed=1 << 20, transcendentals=0),
    )(own, left, right, far)


RING_STEPS = (0, -1, 1, 2)


def channels_kernel(
    first, count, is_first, is_last, shift, left_size, right_size,
    low_r, down, up, high_r, low_l, high_l, lefts, rights, partners, *rest,
):
    rest = list(rest)
    total_in = None if is_first else rest.pop(0)
    out = rest.pop(0)
    source, left_all, right_all = rest[:3]
    rest = rest[3:]
    total, carried = (rest.pop(0), rest.pop(0)) if is_last else (out, None)
    sems = rest.pop(0)
    rsec, lsec = lax.axis_index("rsec"), lax.axis_index("lsec")
    x, z, y, core = rsec // ZN, lax.rem(rsec, ZN), lsec // CORES, lax.rem(lsec, CORES)

    waits = []

    def start(src, dst):
        copy = pltpu.make_async_copy(src, dst, sems.at[len(waits)])
        copy.start()
        waits.append(copy)

    for at, part in enumerate((low_r, down, up, high_r)):
        start(part, source.at[2 * at : 2 * at + 2, 2:6])
    start(low_l, source.at[:, 0:2])
    start(high_l, source.at[:, 6:8])
    ready = []
    for begin, end in ((0, STAGED), (STAGED, count)):
        for step, own, other in zip(RING_STEPS, rights, partners):
            for part, side in ((own, core), (other, 1 - core)):
                row = pl.multiple_of(16 * (CORES * lax.rem(y + step + YN, YN) + side), 16)
                start(
                    part.at[first + begin : first + end],
                    right_all.at[begin:end, :, pl.ds(row, 16)],
                )
        for outer, bundle in zip(RING_STEPS, lefts):
            for at, inner in enumerate(RING_STEPS):
                dx, dz = (outer, inner) if is_first else (inner, outer)
                row = 8 * (ZN * lax.rem(x + dx + XN, XN) + lax.rem(z + dz + ZN, ZN))
                start(
                    bundle.at[at, begin:end],
                    left_all.at[begin:end, :, pl.ds(pl.multiple_of(row, 8), 8)],
                )
        ready.append(len(waits))
    if not is_first:
        start(total_in, carried)

    def add_channels(ks, fresh=False):
        shifts = [(shift[0, first + k], shift[1, first + k]) for k in ks]
        for r in range(4):
            partial = []
            for k, (dl, dr) in zip(ks, shifts):
                rows = source[r + SHIFT - dr, pl.ds(SHIFT - dl, 4)].reshape(4 * 256, 128)
                partial.append(
                    lax.dot_general(
                        rows, right_all[k, r], NT, preferred_element_type=jnp.float32
                    ).astype(jnp.bfloat16)
                )
            for l in range(4):
                added = None
                for at in range(0, len(ks), 2):
                    stacked = jnp.concatenate(
                        [
                            jnp.concatenate(
                                [p[l * 256 : l * 256 + 128], p[l * 256 + 128 : l * 256 + 256]],
                                axis=1,
                            )
                            for p in partial[at : at + 2]
                        ],
                        axis=0,
                    )
                    sides = jnp.concatenate([left_all[k, l] for k in ks[at : at + 2]], axis=1)
                    product = lax.dot_general(
                        sides, stacked, NN, preferred_element_type=jnp.float32
                    )
                    added = product if added is None else added + product
                total[l, r] = added if fresh else total[l, r] + added

    def four_channels(group, carry):
        add_channels([4 * group + j for j in range(4)])
        return carry

    for copy in waits[: ready[0]]:
        copy.wait()
    add_channels(list(range(STAGED)), fresh=True)
    for copy in waits[ready[0] : ready[1]]:
        copy.wait()
    lax.fori_loop(1, count // 4, four_channels, 0)
    if count % 4:
        add_channels(list(range(count // 4 * 4, count)))
    for copy in waits[ready[1] :]:
        copy.wait()

    if is_last:
        row = lax.broadcasted_iota(jnp.int32, (128, 128), 0)
        col = lax.broadcasted_iota(jnp.int32, (128, 128), 1)
        for l in range(4):
            for r in range(4):
                live = (row < left_size[l]) & (col < right_size[r])
                for v in range(2):
                    lanes = slice(v * 128, v * 128 + 128)
                    block = total[l, r, :, lanes] + carried[l, r, :, lanes]
                    out[v, l, :, r * 128 : r * 128 + 128] = jnp.where(live, block, 0.0).astype(
                        jnp.bfloat16
                    )


def run_channels(first, count, is_first, is_last, scalars, sources, lefts, rights, partners, total):
    totals = jax.ShapeDtypeStruct((4, 4, 128, 256), jnp.float32)
    result = jax.ShapeDtypeStruct((2, 4, 128, 512), jnp.bfloat16)
    anywhere = pl.BlockSpec(memory_space=pltpu.HBM)
    smem = pl.BlockSpec(memory_space=pltpu.SMEM)
    operands = [*scalars, *sources, tuple(lefts), tuple(rights), tuple(partners)]
    specs = [smem] * 3 + [anywhere] * 6 + [(anywhere,) * 4] * 3
    if not is_first:
        operands.append(total)
        specs.append(anywhere)
    scratch = [
        pltpu.VMEM((8, 8, 256, 128), jnp.bfloat16),
        pltpu.VMEM((count, 4, 128, 128), jnp.bfloat16),
        pltpu.VMEM((count, 4, 128, 128), jnp.bfloat16),
    ]
    if is_last:
        scratch += [pltpu.VMEM((4, 4, 128, 256), jnp.float32)] * 2
    scratch.append(pltpu.SemaphoreType.DMA((56,)))
    return pl.pallas_call(
        functools.partial(channels_kernel, first, count, is_first, is_last),
        out_shape=result if is_last else totals,
        in_specs=specs,
        out_specs=pl.BlockSpec(memory_space=pltpu.VMEM),
        scratch_shapes=scratch,
        compiler_params=pltpu.CompilerParams(vmem_limit_bytes=60 * 1024 * 1024),
        cost_estimate=pl.CostEstimate(
            flops=count * 4 * 4 * 2 * 2 * 2 * 128**3, bytes_accessed=10 << 20, transcendentals=0
        ),
    )(*operands)


def applied(two_site, left_env, right_env, left_size, right_size, channel_shift):
    steps = (1, -1, 2)
    rights = [right_env] + [lax.ppermute(right_env, "lsec", shifted_y(steps[i])) for i in range(3)]
    part_a, part_b, down, up = prepared(two_site, left_env, left_size, right_size)
    ring_a = [lax.ppermute(part_a, "rsec", shifted_z(steps[i])) for i in range(3)]
    ring_b = [lax.ppermute(part_b, "rsec", shifted_x(steps[i])) for i in range(3)]

    l_up = [(i, i + 1) for i in range(7)]
    l_down = [(i + 1, i) for i in range(7)]
    r_up = [(i, i + 1) for i in range(15)]
    r_down = [(i + 1, i) for i in range(15)]
    low_r = lax.ppermute(up, "rsec", r_up)
    high_r = lax.ppermute(down, "rsec", r_down)

    bundle_a = bundled(part_a, *ring_a)
    lefts_a = [bundle_a] + [lax.ppermute(bundle_a, "rsec", shifted_x(steps[i])) for i in range(3)]
    to_next, to_previous = left_rims(low_r, down, up, high_r)
    low_l = lax.ppermute(to_next, "lsec", l_up)
    high_l = lax.ppermute(to_previous, "lsec", l_down)

    swap = [(i, i ^ 1) for i in range(8)]
    partners = [lax.ppermute(part, "lsec", swap) for part in rights]

    bundle_b = bundled(part_b, *ring_b)
    lefts_b = [bundle_b] + [lax.ppermute(bundle_b, "rsec", shifted_z(steps[i])) for i in range(3)]

    scalars = (channel_shift.T, left_size, right_size)
    sources = (low_r, down, up, high_r, low_l, high_l)
    total = run_channels(0, SPLIT, True, False, scalars, sources, lefts_a, rights, partners, None)
    return run_channels(
        SPLIT, KCH - SPLIT, False, True, scalars, sources, lefts_b, rights, partners, total,
    )


def solution(mesh):
    placed = (
        P(None, "lsec", None, "rsec"),
        P(None, "lsec", "rsec", None),
        P(None, "rsec", "lsec", None),
        P("lsec"),
        P("rsec"),
        P(),
    )
    return jax.shard_map(
        applied, mesh=mesh, in_specs=placed, out_specs=P(None, "lsec", None, "rsec"), check_vma=False
    )
```

profile of v0, /device:TPU:1, one launch (start us, length us, event | category | flops | bytes accessed | tf_op | source)
XLA Modules:
  0.0 124.5 jit_solution(1461832546094065688)
XLA Ops:
  0.0 2.5 %shard_map.64 = (bf16[16,4,8,128]{3,2,1,0:T(8,128)(2,1)}, bf16[18,4,8,128]{3,2,1,0:T(8,128)(2,1)}, bf16[2,4,256,128]{3,2,1,0:T(8,128)(2,1)}, bf16[2,4,256,128]{3,2,1,0:T(8,128)(2,1)}) custom-call(s32[4]{0:T(128)} %left_size.5, s32[4]{0:T(128)} %right_size.5, bf16[2,4,128,512]{3,2,1,0:T(8,128)(2,1)} %two_site.1, bf16[34,4,8,128]{3,2,1,0:T(8,128)(2,1)} %left_env.1), custom_call_target="tpu_custom_call" | custom-call | flops 1048576 | bytes 2097152 | tf_op jit(solution)/shard_map/pallas_call | solution.py:65
  2.6 4.5 %collective-permute-start = (bf16[2,4,256,128]{3,2,1,0:T(8,128)(2,1)}, bf16[2,4,256,128]{3,2,1,0:T(8,128)(2,1)S(1)}, u32[]{:S(2)}, u32[]{:S(2)}) collective-permute-start(bf16[2,4,256,128]{3,2,1,0:T(8,128)(2,1)} %get-tuple-element.11.up), channel_id=1, source_target_pairs={{0,1},{1,2},{2,3},{3,4},{4,5},{5,6},{6,7},{7,8},{8,9},{9,10},{10,1... | collective-permute-start | bytes 1572872 | tf_op jit(solution)/shard_map/ppermute | solution.py:269
  7.1 1.7 %collective-permute-start.17 = (bf16[16,4,8,128]{3,2,1,0:T(8,128)(2,1)}, bf16[16,4,8,128]{3,2,1,0:T(8,128)(2,1)S(1)}, u32[]{:S(2)}, u32[]{:S(2)}) collective-permute-start(bf16[16,4,8,128]{3,2,1,0:T(8,128)(2,1)} %get-tuple-element.16.own), channel_id=1, source_target_pairs={{0,1},{1,2},{2,3},{3,0},{4,5},{5,6},{6,7},{7,4},{8,9},{9,10},{10,1... | collective-permute-start | bytes 393224 | tf_op jit(solution)/shard_map/ppermute | solution.py:262
  8.8 1.1 collective-permute-start.18
  9.8 2.1 %collective-permute-start.19 = (bf16[16,4,8,128]{3,2,1,0:T(8,128)(2,1)}, bf16[16,4,8,128]{3,2,1,0:T(8,128)(2,1)S(1)}, u32[]{:S(2)}, u32[]{:S(2)}) collective-permute-start(bf16[16,4,8,128]{3,2,1,0:T(8,128)(2,1)} %get-tuple-element.16.own), channel_id=1, source_target_pairs={{0,2},{1,3},{2,0},{3,1},{4,6},{5,7},{6,4},{7,5},{8,10},{9,11},{10,... | collective-permute-start | bytes 393224 | tf_op jit(solution)/shard_map/ppermute | solution.py:262
  11.9 1.2 collective-permute-start.4
  13.1 7.7 %collective-permute-done.17.left = bf16[16,4,8,128]{3,2,1,0:T(8,128)(2,1)S(1)} collective-permute-done((bf16[16,4,8,128]{3,2,1,0:T(8,128)(2,1)}, bf16[16,4,8,128]{3,2,1,0:T(8,128)(2,1)S(1)}, u32[]{:S(2)}, u32[]{:S(2)}) %collective-permute-start.17) | collective-permute-done | bytes 131104 | tf_op jit(solution)/shard_map/ppermute | solution.py:262
  20.8 6.7 %collective-permute-start.5 = (bf16[18,4,8,128]{3,2,1,0:T(8,128)(2,1)}, bf16[18,4,8,128]{3,2,1,0:T(8,128)(2,1)S(1)}, u32[]{:S(2)}, u32[]{:S(2)}) collective-permute-start(bf16[18,4,8,128]{3,2,1,0:T(8,128)(2,1)} %get-tuple-element.15.own), channel_id=1, source_target_pairs={{0,12},{1,13},{2,14},{3,15},{4,0},{5,1},{6,2},{7,3},{8,4},{9,5},{1... | collective-permute-start | bytes 442376 | tf_op jit(solution)/shard_map/ppermute | solution.py:263
  27.4 1.3 %collective-permute-start.10 = (bf16[34,4,16,128]{3,2,1,0:T(8,128)(2,1)}, bf16[34,4,16,128]{3,2,1,0:T(8,128)(2,1)S(1)}, u32[]{:S(2)}, u32[]{:S(2)}) collective-permute-start(bf16[34,4,16,128]{3,2,1,0:T(8,128)(2,1)} %rights_0_.3), channel_id=1, source_target_pairs={{0,32},{16,48},{32,64},{48,80},{64,96},{80,112},{96,0},{112,16},{1... | collective-permute-start | bytes 1671176 | tf_op jit(solution)/shard_map/ppermute | solution.py:260
  28.7 1.5 %collective-permute-start.11 = (bf16[34,4,16,128]{3,2,1,0:T(8,128)(2,1)}, bf16[34,4,16,128]{3,2,1,0:T(8,128)(2,1)S(1)}, u32[]{:S(2)}, u32[]{:S(2)}) collective-permute-start(bf16[34,4,16,128]{3,2,1,0:T(8,128)(2,1)} %rights_0_.3), channel_id=1, source_target_pairs={{0,96},{16,112},{32,0},{48,16},{64,32},{80,48},{96,64},{112,80},{1... | collective-permute-start | bytes 1671176 | tf_op jit(solution)/shard_map/ppermute | solution.py:260
  30.3 1.3 %collective-permute-start.1 = (bf16[2,4,256,128]{3,2,1,0:T(8,128)(2,1)}, bf16[2,4,256,128]{3,2,1,0:T(8,128)(2,1)S(1)}, u32[]{:S(2)}, u32[]{:S(2)}) collective-permute-start(bf16[2,4,256,128]{3,2,1,0:T(8,128)(2,1)} %get-tuple-element.12.down), channel_id=1, source_target_pairs={{1,0},{2,1},{3,2},{4,3},{5,4},{6,5},{7,6},{8,7},{9,8},{10,9},{11,1... | collective-permute-start | bytes 1572872 | tf_op jit(solution)/shard_map/ppermute | solution.py:270
  31.6 3.4 %collective-permute-start.6 = (bf16[18,4,8,128]{3,2,1,0:T(8,128)(2,1)}, bf16[18,4,8,128]{3,2,1,0:T(8,128)(2,1)S(1)}, u32[]{:S(2)}, u32[]{:S(2)}) collective-permute-start(bf16[18,4,8,128]{3,2,1,0:T(8,128)(2,1)} %get-tuple-element.15.own), channel_id=1, source_target_pairs={{0,8},{1,9},{2,10},{3,11},{4,12},{5,13},{6,14},{7,15},{8,0},{9,1},... | collective-permute-start | bytes 442376 | tf_op jit(solution)/shard_map/ppermute | solution.py:263
  35.0 2.7 %collective-permute-done.6.far = bf16[18,4,8,128]{3,2,1,0:T(8,128)(2,1)S(1)} collective-permute-done((bf16[18,4,8,128]{3,2,1,0:T(8,128)(2,1)}, bf16[18,4,8,128]{3,2,1,0:T(8,128)(2,1)S(1)}, u32[]{:S(2)}, u32[]{:S(2)}) %collective-permute-start.6) | collective-permute-done | bytes 147488 | tf_op jit(solution)/shard_map/ppermute | solution.py:263
  37.7 1.2 collective-permute-start.12
  39.0 3.0 %collective-permute-start.13 = (bf16[34,4,16,128]{3,2,1,0:T(8,128)(2,1)}, bf16[34,4,16,128]{3,2,1,0:T(8,128)(2,1)S(1)}, u32[]{:S(2)}, u32[]{:S(2)}) collective-permute-start(bf16[34,4,16,128]{3,2,1,0:T(8,128)(2,1)} %rights_0_.3), channel_id=1, source_target_pairs={{0,16},{16,0},{32,48},{48,32},{64,80},{80,64},{96,112},{112,96},{1... | collective-permute-start | bytes 1671176 | tf_op jit(solution)/shard_map/ppermute | solution.py:279
  42.0 0.9 copy-done.7
  43.0 1.0 collective-permute-done.1.high_r
  44.0 9.1 %collective-permute-start.20 = (bf16[4,16,4,8,128]{4,3,2,1,0:T(8,128)(2,1)S(1)}, bf16[4,16,4,8,128]{4,3,2,1,0:T(8,128)(2,1)S(1)}, u32[]{:S(2)}, u32[]{:S(2)}) collective-permute-start(bf16[4,16,4,8,128]{4,3,2,1,0:T(8,128)(2,1)S(1)} %shard_map.67.lefts_0_), channel_id=1, source_target_pairs={{0,4},{1,5},{2,6},{3,7},{4,8},{5,9},{6,10},{7,11},{8,12},{9,13},{1... | collective-permute-start | bytes 1572872 | tf_op jit(solution)/shard_map/ppermute | solution.py:273
  53.1 1.9 %collective-permute-start.21 = (bf16[4,16,4,8,128]{4,3,2,1,0:T(8,128)(2,1)S(1)}, bf16[4,16,4,8,128]{4,3,2,1,0:T(8,128)(2,1)S(1)}, u32[]{:S(2)}, u32[]{:S(2)}) collective-permute-start(bf16[4,16,4,8,128]{4,3,2,1,0:T(8,128)(2,1)S(1)} %shard_map.67.lefts_0_), channel_id=1, source_target_pairs={{0,12},{1,13},{2,14},{3,15},{4,0},{5,1},{6,2},{7,3},{8,4},{9,5},{1... | collective-permute-start | bytes 1572872 | tf_op jit(solution)/shard_map/ppermute | solution.py:273
  55.0 1.2 collective-permute-start.22
  56.2 1.0 copy-done.2
  57.2 1.0 copy-done.3
  58.4 2.9 %collective-permute-start.2 = (bf16[8,2,256,128]{3,2,1,0:T(8,128)(2,1)S(1)}, bf16[8,2,256,128]{3,2,1,0:T(8,128)(2,1)S(1)}, u32[]{:S(2)}, u32[]{:S(2)}) collective-permute-start(bf16[8,2,256,128]{3,2,1,0:T(8,128)(2,1)S(1)} %get-tuple-element.13), channel_id=1, source_target_pairs={{0,16},{16,32},{32,48},{48,64},{64,80},{80,96},{96,112},{1,17},{17... | collective-permute-start | bytes 3145736 | tf_op jit(solution)/shard_map/ppermute | solution.py:275
  61.4 2.5 %collective-permute-start.3 = (bf16[8,2,256,128]{3,2,1,0:T(8,128)(2,1)S(1)}, bf16[8,2,256,128]{3,2,1,0:T(8,128)(2,1)S(1)}, u32[]{:S(2)}, u32[]{:S(2)}) collective-permute-start(bf16[8,2,256,128]{3,2,1,0:T(8,128)(2,1)S(1)} %get-tuple-element.14), channel_id=1, source_target_pairs={{16,0},{32,16},{48,32},{64,48},{80,64},{96,80},{112,96},{17,1},{33... | collective-permute-start | bytes 3145736 | tf_op jit(solution)/shard_map/ppermute | solution.py:276
  63.9 3.1 %collective-permute-done.20.lefts_1_ = bf16[4,16,4,8,128]{4,3,2,1,0:T(8,128)(2,1)S(1)} collective-permute-done((bf16[4,16,4,8,128]{4,3,2,1,0:T(8,128)(2,1)S(1)}, bf16[4,16,4,8,128]{4,3,2,1,0:T(8,128)(2,1)S(1)}, u32[]{:S(2)}, u32[]{:S(2)}) %collective-permute-start.20) | collective-permute-done | bytes 524320 | tf_op jit(solution)/shard_map/ppermute | solution.py:273
  67.8 10.6 %collective-permute-start.15 = (bf16[34,4,16,128]{3,2,1,0:T(8,128)(2,1)S(1)}, bf16[34,4,16,128]{3,2,1,0:T(8,128)(2,1)S(1)}, u32[]{:S(2)}, u32[]{:S(2)}) collective-permute-start(bf16[34,4,16,128]{3,2,1,0:T(8,128)(2,1)S(1)} %collective-permute-done.11.rights_2_), channel_id=1, source_target_pairs={{0,16},{16,0},{32,48},{48,32},{64,80},{80,64},{96,112},{112,96},{1... | collective-permute-start | bytes 1671176 | tf_op jit(solution)/shard_map/ppermute | solution.py:279
  79.2 1.0 collective-permute-start.16
  80.4 2.6 %collective-permute-start.8 = (bf16[4,18,4,8,128]{4,3,2,1,0:T(8,128)(2,1)S(1)}, bf16[4,18,4,8,128]{4,3,2,1,0:T(8,128)(2,1)}, u32[]{:S(2)}, u32[]{:S(2)}) collective-permute-start(bf16[4,18,4,8,128]{4,3,2,1,0:T(8,128)(2,1)S(1)} %shard_map.66.lefts_0_), channel_id=1, source_target_pairs={{0,3},{1,0},{2,1},{3,2},{4,7},{5,4},{6,5},{7,6},{8,11},{9,8},{10,9... | collective-permute-start | bytes 1769480 | tf_op jit(solution)/shard_map/ppermute | solution.py:282
  83.8 1.0 copy-done.9
  84.9 13.2 %shard_map.68.rest_0_ = f32[4,4,128,256]{3,2,1,0:T(8,128)} custom-call(s32[2,34]{1,0:T(2,128)} %bitcast.1, s32[4]{0:T(128)} %left_size.5, s32[4]{0:T(128)} %right_size.5, bf16[2,4,256,128]{3,2,1,0:T(8,128)(2,1)} %copy-done.4, bf16[2,4,256,128]{3,2,1,0:T(8,128)(2,1)} %get-tuple-element.12.down, bf16[2,4,256,128]{3,2,1,0:T(8,128)(2,1)} %get-tuple-element.11.up, ...), custom_call_target="tpu_custom_call" | custom-call | flops 4294967296 | bytes 10485760 | tf_op jit(solution)/shard_map/pallas_call | solution.py:245
  98.1 11.0 %collective-permute-done.7.lefts_1_ = bf16[4,18,4,8,128]{4,3,2,1,0:T(8,128)(2,1)S(1)} collective-permute-done((bf16[4,18,4,8,128]{4,3,2,1,0:T(8,128)(2,1)S(1)}, bf16[4,18,4,8,128]{4,3,2,1,0:T(8,128)(2,1)S(1)}, u32[]{:S(2)}, u32[]{:S(2)}) %collective-permute-start.7) | collective-permute-done | bytes 589856 | tf_op jit(solution)/shard_map/ppermute | solution.py:282
  109.9 14.4 %shard_map.69 = bf16[2,4,128,512]{3,2,1,0:T(8,128)(2,1)} custom-call(s32[2,34]{1,0:T(2,128)} %bitcast.2, s32[4]{0:T(128)} %left_size.5, s32[4]{0:T(128)} %right_size.5, bf16[2,4,256,128]{3,2,1,0:T(8,128)(2,1)} %copy-done.4, bf16[2,4,256,128]{3,2,1,0:T(8,128)(2,1)} %get-tuple-element.12.down, bf16[2,4,256,128]{3,2,1,0:T(8,128)(2,1)} %get-tuple-element.11.up, ...), custom_call_target="tpu_custom_call" | custom-call | flops 4831838208 | bytes 10485760 | tf_op jit(solution)/shard_map/pallas_call | solution.py:245
  (62 shorter events, 3.4 us)
Async XLA Ops:
  2.5 77.6 %copy-start.6 = (bf16[18,4,8,128]{3,2,1,0:T(8,128)(2,1)S(1)}, bf16[18,4,8,128]{3,2,1,0:T(8,128)(2,1)}, u32[]{:S(2)}) copy-start(bf16[18,4,8,128]{3,2,1,0:T(8,128)(2,1)} %get-tuple-element.15.own) | copy-start | bytes 442372
  2.6 36.4 %collective-permute-start = (bf16[2,4,256,128]{3,2,1,0:T(8,128)(2,1)}, bf16[2,4,256,128]{3,2,1,0:T(8,128)(2,1)S(1)}, u32[]{:S(2)}, u32[]{:S(2)}) collective-permute-start(bf16[2,4,256,128]{3,2,1,0:T(8,128)(2,1)} %get-tuple-element.11.up), channel_id=1, source_target_pairs={{0,1},{1,2},{2,3},{3,4},{4,5},{5,6},{6,7},{7,8},{8,9},{9,10},{10,1... | collective-permute-start | bytes 1572872 | tf_op jit(solution)/shard_map/ppermute | solution.py:269
  7.1 13.7 %collective-permute-start.17 = (bf16[16,4,8,128]{3,2,1,0:T(8,128)(2,1)}, bf16[16,4,8,128]{3,2,1,0:T(8,128)(2,1)S(1)}, u32[]{:S(2)}, u32[]{:S(2)}) collective-permute-start(bf16[16,4,8,128]{3,2,1,0:T(8,128)(2,1)} %get-tuple-element.16.own), channel_id=1, source_target_pairs={{0,1},{1,2},{2,3},{3,0},{4,5},{5,6},{6,7},{7,4},{8,9},{9,10},{10,1... | collective-permute-start | bytes 393224 | tf_op jit(solution)/shard_map/ppermute | solution.py:262
  8.8 18.7 %collective-permute-start.18 = (bf16[16,4,8,128]{3,2,1,0:T(8,128)(2,1)}, bf16[16,4,8,128]{3,2,1,0:T(8,128)(2,1)S(1)}, u32[]{:S(2)}, u32[]{:S(2)}) collective-permute-start(bf16[16,4,8,128]{3,2,1,0:T(8,128)(2,1)} %get-tuple-element.16.own), channel_id=1, source_target_pairs={{0,3},{1,0},{2,1},{3,2},{4,7},{5,4},{6,5},{7,6},{8,11},{9,8},{10,9... | collective-permute-start | bytes 393224 | tf_op jit(solution)/shard_map/ppermute | solution.py:262
  9.8 18.9 %collective-permute-start.19 = (bf16[16,4,8,128]{3,2,1,0:T(8,128)(2,1)}, bf16[16,4,8,128]{3,2,1,0:T(8,128)(2,1)S(1)}, u32[]{:S(2)}, u32[]{:S(2)}) collective-permute-start(bf16[16,4,8,128]{3,2,1,0:T(8,128)(2,1)} %get-tuple-element.16.own), channel_id=1, source_target_pairs={{0,2},{1,3},{2,0},{3,1},{4,6},{5,7},{6,4},{7,5},{8,10},{9,11},{10,... | collective-permute-start | bytes 393224 | tf_op jit(solution)/shard_map/ppermute | solution.py:262
  11.9 18.4 %collective-permute-start.4 = (bf16[18,4,8,128]{3,2,1,0:T(8,128)(2,1)}, bf16[18,4,8,128]{3,2,1,0:T(8,128)(2,1)S(1)}, u32[]{:S(2)}, u32[]{:S(2)}) collective-permute-start(bf16[18,4,8,128]{3,2,1,0:T(8,128)(2,1)} %get-tuple-element.15.own), channel_id=1, source_target_pairs={{0,4},{1,5},{2,6},{3,7},{4,8},{5,9},{6,10},{7,11},{8,12},{9,13},{1... | collective-permute-start | bytes 442376 | tf_op jit(solution)/shard_map/ppermute | solution.py:263
  20.8 10.8 %collective-permute-start.5 = (bf16[18,4,8,128]{3,2,1,0:T(8,128)(2,1)}, bf16[18,4,8,128]{3,2,1,0:T(8,128)(2,1)S(1)}, u32[]{:S(2)}, u32[]{:S(2)}) collective-permute-start(bf16[18,4,8,128]{3,2,1,0:T(8,128)(2,1)} %get-tuple-element.15.own), channel_id=1, source_target_pairs={{0,12},{1,13},{2,14},{3,15},{4,0},{5,1},{6,2},{7,3},{8,4},{9,5},{1... | collective-permute-start | bytes 442376 | tf_op jit(solution)/shard_map/ppermute | solution.py:263
  27.4 25.7 %collective-permute-start.10 = (bf16[34,4,16,128]{3,2,1,0:T(8,128)(2,1)}, bf16[34,4,16,128]{3,2,1,0:T(8,128)(2,1)S(1)}, u32[]{:S(2)}, u32[]{:S(2)}) collective-permute-start(bf16[34,4,16,128]{3,2,1,0:T(8,128)(2,1)} %rights_0_.3), channel_id=1, source_target_pairs={{0,32},{16,48},{32,64},{48,80},{64,96},{80,112},{96,0},{112,16},{1... | collective-permute-start | bytes 1671176 | tf_op jit(solution)/shard_map/ppermute | solution.py:260
  28.7 26.3 %collective-permute-start.11 = (bf16[34,4,16,128]{3,2,1,0:T(8,128)(2,1)}, bf16[34,4,16,128]{3,2,1,0:T(8,128)(2,1)S(1)}, u32[]{:S(2)}, u32[]{:S(2)}) collective-permute-start(bf16[34,4,16,128]{3,2,1,0:T(8,128)(2,1)} %rights_0_.3), channel_id=1, source_target_pairs={{0,96},{16,112},{32,0},{48,16},{64,32},{80,48},{96,64},{112,80},{1... | collective-permute-start | bytes 1671176 | tf_op jit(solution)/shard_map/ppermute | solution.py:260
  30.3 13.8 %collective-permute-start.1 = (bf16[2,4,256,128]{3,2,1,0:T(8,128)(2,1)}, bf16[2,4,256,128]{3,2,1,0:T(8,128)(2,1)S(1)}, u32[]{:S(2)}, u32[]{:S(2)}) collective-permute-start(bf16[2,4,256,128]{3,2,1,0:T(8,128)(2,1)} %get-tuple-element.12.down), channel_id=1, source_target_pairs={{1,0},{2,1},{3,2},{4,3},{5,4},{6,5},{7,6},{8,7},{9,8},{10,9},{11,1... | collective-permute-start | bytes 1572872 | tf_op jit(solution)/shard_map/ppermute | solution.py:270
  31.6 6.2 %collective-permute-start.6 = (bf16[18,4,8,128]{3,2,1,0:T(8,128)(2,1)}, bf16[18,4,8,128]{3,2,1,0:T(8,128)(2,1)S(1)}, u32[]{:S(2)}, u32[]{:S(2)}) collective-permute-start(bf16[18,4,8,128]{3,2,1,0:T(8,128)(2,1)} %get-tuple-element.15.own), channel_id=1, source_target_pairs={{0,8},{1,9},{2,10},{3,11},{4,12},{5,13},{6,14},{7,15},{8,0},{9,1},... | collective-permute-start | bytes 442376 | tf_op jit(solution)/shard_map/ppermute | solution.py:263
  37.7 20.7 %collective-permute-start.12 = (bf16[34,4,16,128]{3,2,1,0:T(8,128)(2,1)}, bf16[34,4,16,128]{3,2,1,0:T(8,128)(2,1)S(1)}, u32[]{:S(2)}, u32[]{:S(2)}) collective-permute-start(bf16[34,4,16,128]{3,2,1,0:T(8,128)(2,1)} %rights_0_.3), channel_id=1, source_target_pairs={{0,64},{16,80},{32,96},{48,112},{64,0},{80,16},{96,32},{112,48},{1... | collective-permute-start | bytes 1671176 | tf_op jit(solution)/shard_map/ppermute | solution.py:260
  39.0 41.2 %copy-start.4 = (bf16[2,4,256,128]{3,2,1,0:T(8,128)(2,1)}, bf16[2,4,256,128]{3,2,1,0:T(8,128)(2,1)S(1)}, u32[]{:S(2)}) copy-start(bf16[2,4,256,128]{3,2,1,0:T(8,128)(2,1)S(1)} %collective-permute-done.low_r) | copy-start | bytes 1572868
  39.0 22.3 %collective-permute-start.13 = (bf16[34,4,16,128]{3,2,1,0:T(8,128)(2,1)}, bf16[34,4,16,128]{3,2,1,0:T(8,128)(2,1)S(1)}, u32[]{:S(2)}, u32[]{:S(2)}) collective-permute-start(bf16[34,4,16,128]{3,2,1,0:T(8,128)(2,1)} %rights_0_.3), channel_id=1, source_target_pairs={{0,16},{16,0},{32,48},{48,32},{64,80},{80,64},{96,112},{112,96},{1... | collective-permute-start | bytes 1671176 | tf_op jit(solution)/shard_map/ppermute | solution.py:279
  43.0 41.9 %copy-start.1 = (bf16[4,16,4,8,128]{4,3,2,1,0:T(8,128)(2,1)}, bf16[4,16,4,8,128]{4,3,2,1,0:T(8,128)(2,1)S(1)}, u32[]{:S(2)}) copy-start(bf16[4,16,4,8,128]{4,3,2,1,0:T(8,128)(2,1)S(1)} %shard_map.67.lefts_0_) | copy-start | bytes 1572868
  44.0 40.9 %copy-start.5 = (bf16[2,4,256,128]{3,2,1,0:T(8,128)(2,1)}, bf16[2,4,256,128]{3,2,1,0:T(8,128)(2,1)S(1)}, u32[]{:S(2)}) copy-start(bf16[2,4,256,128]{3,2,1,0:T(8,128)(2,1)S(1)} %collective-permute-done.1.high_r) | copy-start | bytes 1572868
  44.0 23.0 %collective-permute-start.20 = (bf16[4,16,4,8,128]{4,3,2,1,0:T(8,128)(2,1)S(1)}, bf16[4,16,4,8,128]{4,3,2,1,0:T(8,128)(2,1)S(1)}, u32[]{:S(2)}, u32[]{:S(2)}) collective-permute-start(bf16[4,16,4,8,128]{4,3,2,1,0:T(8,128)(2,1)S(1)} %shard_map.67.lefts_0_), channel_id=1, source_target_pairs={{0,4},{1,5},{2,6},{3,7},{4,8},{5,9},{6,10},{7,11},{8,12},{9,13},{1... | collective-permute-start | bytes 1572872 | tf_op jit(solution)/shard_map/ppermute | solution.py:273
  53.1 29.9 %copy-start.11 = (bf16[34,4,16,128]{3,2,1,0:T(8,128)(2,1)}, bf16[34,4,16,128]{3,2,1,0:T(8,128)(2,1)S(1)}, u32[]{:S(2)}) copy-start(bf16[34,4,16,128]{3,2,1,0:T(8,128)(2,1)S(1)} %collective-permute-done.10.rights_1_) | copy-start | bytes 1671172
  53.1 14.6 %collective-permute-start.21 = (bf16[4,16,4,8,128]{4,3,2,1,0:T(8,128)(2,1)S(1)}, bf16[4,16,4,8,128]{4,3,2,1,0:T(8,128)(2,1)S(1)}, u32[]{:S(2)}, u32[]{:S(2)}) collective-permute-start(bf16[4,16,4,8,128]{4,3,2,1,0:T(8,128)(2,1)S(1)} %shard_map.67.lefts_0_), channel_id=1, source_target_pairs={{0,12},{1,13},{2,14},{3,15},{4,0},{5,1},{6,2},{7,3},{8,4},{9,5},{1... | collective-permute-start | bytes 1572872 | tf_op jit(solution)/shard_map/ppermute | solution.py:273
  55.0 28.1 %copy-start.12 = (bf16[34,4,16,128]{3,2,1,0:T(8,128)(2,1)}, bf16[34,4,16,128]{3,2,1,0:T(8,128)(2,1)S(1)}, u32[]{:S(2)}) copy-start(bf16[34,4,16,128]{3,2,1,0:T(8,128)(2,1)S(1)} %collective-permute-done.11.rights_2_) | copy-start | bytes 1671172
  55.0 24.2 %collective-permute-start.22 = (bf16[4,16,4,8,128]{4,3,2,1,0:T(8,128)(2,1)S(1)}, bf16[4,16,4,8,128]{4,3,2,1,0:T(8,128)(2,1)S(1)}, u32[]{:S(2)}, u32[]{:S(2)}) collective-permute-start(bf16[4,16,4,8,128]{4,3,2,1,0:T(8,128)(2,1)S(1)} %shard_map.67.lefts_0_), channel_id=1, source_target_pairs={{0,8},{1,9},{2,10},{3,11},{4,12},{5,13},{6,14},{7,15},{8,0},{9,1},... | collective-permute-start | bytes 1572872 | tf_op jit(solution)/shard_map/ppermute | solution.py:273
  58.4 24.7 %copy-start.13 = (bf16[34,4,16,128]{3,2,1,0:T(8,128)(2,1)}, bf16[34,4,16,128]{3,2,1,0:T(8,128)(2,1)S(1)}, u32[]{:S(2)}) copy-start(bf16[34,4,16,128]{3,2,1,0:T(8,128)(2,1)S(1)} %collective-permute-done.12.rights_3_) | copy-start | bytes 1671172
  58.4 24.6 %collective-permute-start.2 = (bf16[8,2,256,128]{3,2,1,0:T(8,128)(2,1)S(1)}, bf16[8,2,256,128]{3,2,1,0:T(8,128)(2,1)S(1)}, u32[]{:S(2)}, u32[]{:S(2)}) collective-permute-start(bf16[8,2,256,128]{3,2,1,0:T(8,128)(2,1)S(1)} %get-tuple-element.13), channel_id=1, source_target_pairs={{0,16},{16,32},{32,48},{48,64},{64,80},{80,96},{96,112},{1,17},{17... | collective-permute-start | bytes 3145736 | tf_op jit(solution)/shard_map/ppermute | solution.py:275
  61.3 21.7 %copy-start.14 = (bf16[34,4,16,128]{3,2,1,0:T(8,128)(2,1)}, bf16[34,4,16,128]{3,2,1,0:T(8,128)(2,1)S(1)}, u32[]{:S(2)}) copy-start(bf16[34,4,16,128]{3,2,1,0:T(8,128)(2,1)S(1)} %collective-permute-done.13.partners_0_) | copy-start | bytes 1671172
  61.4 21.7 %collective-permute-start.3 = (bf16[8,2,256,128]{3,2,1,0:T(8,128)(2,1)S(1)}, bf16[8,2,256,128]{3,2,1,0:T(8,128)(2,1)S(1)}, u32[]{:S(2)}, u32[]{:S(2)}) collective-permute-start(bf16[8,2,256,128]{3,2,1,0:T(8,128)(2,1)S(1)} %get-tuple-element.14), channel_id=1, source_target_pairs={{16,0},{32,16},{48,32},{64,48},{80,64},{96,80},{112,96},{17,1},{33... | collective-permute-start | bytes 3145736 | tf_op jit(solution)/shard_map/ppermute | solution.py:276
  67.0 13.2 %collective-permute-start.14 = (bf16[34,4,16,128]{3,2,1,0:T(8,128)(2,1)S(1)}, bf16[34,4,16,128]{3,2,1,0:T(8,128)(2,1)S(1)}, u32[]{:S(2)}, u32[]{:S(2)}) collective-permute-start(bf16[34,4,16,128]{3,2,1,0:T(8,128)(2,1)S(1)} %collective-permute-done.10.rights_1_), channel_id=1, source_target_pairs={{0,16},{16,0},{32,48},{48,32},{64,80},{80,64},{96,112},{112,96},{1... | collective-permute-start | bytes 1671176 | tf_op jit(solution)/shard_map/ppermute | solution.py:279
  67.8 12.6 %collective-permute-start.15 = (bf16[34,4,16,128]{3,2,1,0:T(8,128)(2,1)S(1)}, bf16[34,4,16,128]{3,2,1,0:T(8,128)(2,1)S(1)}, u32[]{:S(2)}, u32[]{:S(2)}) collective-permute-start(bf16[34,4,16,128]{3,2,1,0:T(8,128)(2,1)S(1)} %collective-permute-done.11.rights_2_), channel_id=1, source_target_pairs={{0,16},{16,0},{32,48},{48,32},{64,80},{80,64},{96,112},{112,96},{1... | collective-permute-start | bytes 1671176 | tf_op jit(solution)/shard_map/ppermute | solution.py:279
  79.2 3.9 %collective-permute-start.16 = (bf16[34,4,16,128]{3,2,1,0:T(8,128)(2,1)S(1)}, bf16[34,4,16,128]{3,2,1,0:T(8,128)(2,1)S(1)}, u32[]{:S(2)}, u32[]{:S(2)}) collective-permute-start(bf16[34,4,16,128]{3,2,1,0:T(8,128)(2,1)S(1)} %collective-permute-done.12.rights_3_), channel_id=1, source_target_pairs={{0,16},{16,0},{32,48},{48,32},{64,80},{80,64},{96,112},{112,96},{1... | collective-permute-start | bytes 1671176 | tf_op jit(solution)/shard_map/ppermute | solution.py:279
  80.2 17.8 %copy-start = (bf16[4,18,4,8,128]{4,3,2,1,0:T(8,128)(2,1)}, bf16[4,18,4,8,128]{4,3,2,1,0:T(8,128)(2,1)S(1)}, u32[]{:S(2)}) copy-start(bf16[4,18,4,8,128]{4,3,2,1,0:T(8,128)(2,1)S(1)} %shard_map.66.lefts_0_) | copy-start | bytes 1769476
  80.3 28.8 %collective-permute-start.7 = (bf16[4,18,4,8,128]{4,3,2,1,0:T(8,128)(2,1)S(1)}, bf16[4,18,4,8,128]{4,3,2,1,0:T(8,128)(2,1)S(1)}, u32[]{:S(2)}, u32[]{:S(2)}) collective-permute-start(bf16[4,18,4,8,128]{4,3,2,1,0:T(8,128)(2,1)S(1)} %shard_map.66.lefts_0_), channel_id=1, source_target_pairs={{0,1},{1,2},{2,3},{3,0},{4,5},{5,6},{6,7},{7,4},{8,9},{9,10},{10,1... | collective-permute-start | bytes 1769480 | tf_op jit(solution)/shard_map/ppermute | solution.py:282
  80.4 28.7 %collective-permute-start.8 = (bf16[4,18,4,8,128]{4,3,2,1,0:T(8,128)(2,1)S(1)}, bf16[4,18,4,8,128]{4,3,2,1,0:T(8,128)(2,1)}, u32[]{:S(2)}, u32[]{:S(2)}) collective-permute-start(bf16[4,18,4,8,128]{4,3,2,1,0:T(8,128)(2,1)S(1)} %shard_map.66.lefts_0_), channel_id=1, source_target_pairs={{0,3},{1,0},{2,1},{3,2},{4,7},{5,4},{6,5},{7,6},{8,11},{9,8},{10,9... | collective-permute-start | bytes 1769480 | tf_op jit(solution)/shard_map/ppermute | solution.py:282
  83.0 26.0 %collective-permute-start.9 = (bf16[4,18,4,8,128]{4,3,2,1,0:T(8,128)(2,1)S(1)}, bf16[4,18,4,8,128]{4,3,2,1,0:T(8,128)(2,1)}, u32[]{:S(2)}, u32[]{:S(2)}) collective-permute-start(bf16[4,18,4,8,128]{4,3,2,1,0:T(8,128)(2,1)S(1)} %shard_map.66.lefts_0_), channel_id=1, source_target_pairs={{0,2},{1,3},{2,0},{3,1},{4,6},{5,7},{6,4},{7,5},{8,10},{9,11},{10,... | collective-permute-start | bytes 1769480 | tf_op jit(solution)/shard_map/ppermute | solution.py:282
  (12 other events, 48.5 us)
where the time goes:
time: 125 us; the launch traced here: 124 us
  starting transfers between devices  61.7 us (49%)
  Pallas kernels  30.4 us (24%)
  waiting for transfers between devices  26.4 us (21%)
  local copies, waits for them, and re-layouts  5.59 us (4%)
    pallas_call x2, Pallas kernels, run_channels(): pl.pallas_call(functools.partial(channels_kernel, first, count, is_first,...  27.6 us
    ppermute x4, starting transfers between devices, applied(): partners = [lax.ppermute(part, 'lsec', swap) for part in rights]  15.4 us
    ppermute x3, starting transfers between devices, applied(): lax.ppermute(bundle_a, 'rsec', shifted_x(steps[i]))  12.2 us
    ppermute x3, starting transfers between devices, applied(): lax.ppermute(part_b, 'rsec', shifted_x(steps[i]))  11.3 us
    ppermute x3, waiting for transfers between devices, applied(): lax.ppermute(bundle_b, 'rsec', shifted_z(steps[i]))  11 us
    ppermute x3, waiting for transfers between devices, applied(): lax.ppermute(part_a, 'rsec', shifted_z(steps[i]))  7.66 us
    unnamed x42, local copies, waits for them, and re-layouts  5.59 us
    ppermute x3, starting transfers between devices, applied(): lax.ppermute(part_a, 'rsec', shifted_z(steps[i]))  4.81 us
  transfers between devices with their start and end apart: 23, of which 6 were waited for; matrix products, arithmetic and copies ran while one was open for 0% of the time, Pallas kernels for 11%

commit v1 on v0

--- a/solution.py
+++ b/solution.py
@@ -127,7 +127,8 @@
     out = rest.pop(0)
     source, left_all, right_all = rest[:3]
     rest = rest[3:]
-    total, carried = (rest.pop(0), rest.pop(0)) if is_last else (out, None)
+    total = rest.pop(0)
+    carried = rest.pop(0) if is_last else None
     sems = rest.pop(0)
     rsec, lsec = lax.axis_index("rsec"), lax.axis_index("lsec")
     x, z, y, core = rsec // ZN, lax.rem(rsec, ZN), lsec // CORES, lax.rem(lsec, CORES)
@@ -164,7 +165,7 @@
     if not is_first:
         start(total_in, carried)
 
-    def add_channels(ks, fresh=False):
+    def add_channels(ks, fresh=False, finish=None, after_column=None):
         shifts = [(shift[0, first + k], shift[1, first + k]) for k in ks]
         for r in range(4):
             partial = []
@@ -193,7 +194,13 @@
                         sides, stacked, NN, preferred_element_type=jnp.float32
                     )
                     added = product if added is None else added + product
-                total[l, r] = added if fresh else total[l, r] + added
+                value = added if fresh else total[l, r] + added
+                if finish is None:
+                    total[l, r] = value
+                else:
+                    finish(l, r, value)
+            if after_column is not None:
+                after_column(r)
 
     def four_channels(group, carry):
         add_channels([4 * group + j for j in range(4)])
@@ -204,24 +211,38 @@
     add_channels(list(range(STAGED)), fresh=True)
     for copy in waits[ready[0] : ready[1]]:
         copy.wait()
-    lax.fori_loop(1, count // 4, four_channels, 0)
-    if count % 4:
-        add_channels(list(range(count // 4 * 4, count)))
+    final = count // 4 * 4 if count % 4 else count - 4
+    lax.fori_loop(1, final // 4, four_channels, 0)
+    last_ks = list(range(final, count))
     for copy in waits[ready[1] :]:
         copy.wait()
 
-    if is_last:
-        row = lax.broadcasted_iota(jnp.int32, (128, 128), 0)
-        col = lax.broadcasted_iota(jnp.int32, (128, 128), 1)
-        for l in range(4):
-            for r in range(4):
-                live = (row < left_size[l]) & (col < right_size[r])
-                for v in range(2):
-                    lanes = slice(v * 128, v * 128 + 128)
-                    block = total[l, r, :, lanes] + carried[l, r, :, lanes]
-                    out[v, l, :, r * 128 : r * 128 + 128] = jnp.where(live, block, 0.0).astype(
-                        jnp.bfloat16
-                    )
+    if not is_last:
+        flushes = [
+            pltpu.make_async_copy(total.at[:, r], out.at[:, r], sems.at[r]) for r in range(4)
+        ]
+
+        def after_column(r):
+            if r > 0:
+                flushes[r - 1].start()
+
+        add_channels(last_ks, after_column=after_column)
+        flushes[3].start()
+        for copy in flushes:
+            copy.wait()
+        return
+
+    row = lax.broadcasted_iota(jnp.int32, (128, 128), 0)
+    col = lax.broadcasted_iota(jnp.int32, (128, 128), 1)
+
+    def finish(l, r, value):
+        live = (row < left_size[l]) & (col < right_size[r])
+        for v in range(2):
+            lanes = slice(v * 128, v * 128 + 128)
+            block = value[:, lanes] + carried[l, r, :, lanes]
+            out[v, l, :, r * 128 : r * 128 + 128] = jnp.where(live, block, 0.0).astype(jnp.bfloat16)
+
+    add_channels(last_ks, finish=finish)
 
 
 def run_channels(first, count, is_first, is_last, scalars, sources, lefts, rights, partners, total):
@@ -239,14 +260,13 @@
         pltpu.VMEM((count, 4, 128, 128), jnp.bfloat16),
         pltpu.VMEM((count, 4, 128, 128), jnp.bfloat16),
     ]
-    if is_last:
-        scratch += [pltpu.VMEM((4, 4, 128, 256), jnp.float32)] * 2
+    scratch += [pltpu.VMEM((4, 4, 128, 256), jnp.float32)] * (2 if is_last else 1)
     scratch.append(pltpu.SemaphoreType.DMA((56,)))
     return pl.pallas_call(
         functools.partial(channels_kernel, first, count, is_first, is_last),
         out_shape=result if is_last else totals,
         in_specs=specs,
-        out_specs=pl.BlockSpec(memory_space=pltpu.VMEM),
+        out_specs=pl.BlockSpec(memory_space=pltpu.VMEM) if is_last else anywhere,
         scratch_shapes=scratch,
         compiler_params=pltpu.CompilerParams(vmem_limit_bytes=60 * 1024 * 1024),
         cost_estimate=pl.CostEstimate(

time: 125 us -> 125 us (level)
  transfers between devices with their start and end apart: 23 -> 23, of which waited for: 6 -> 6; matrix products, arithmetic and copies ran while one was open for 0% -> 0% of each run, Pallas kernels for 11% -> 10%
where the time goes in v1:
time: 125 us; the launch traced here: 124 us
  starting transfers between devices  61.7 us (49%)
  Pallas kernels  29.7 us (24%)
  waiting for transfers between devices  26.8 us (21%)
  local copies, waits for them, and re-layouts  5.59 us (4%)
    pallas_call x2, Pallas kernels, run_channels(): pl.pallas_call(functools.partial(channels_kernel, first, count, is_first,...  26.9 us
    ppermute x4, starting transfers between devices, applied(): partners = [lax.ppermute(part, 'lsec', swap) for part in rights]  15.4 us
    ppermute x3, starting transfers between devices, applied(): lax.ppermute(bundle_a, 'rsec', shifted_x(steps[i]))  12.2 us
    ppermute x3, waiting for transfers between devices, applied(): lax.ppermute(bundle_b, 'rsec', shifted_z(steps[i]))  11.4 us
    ppermute x3, starting transfers between devices, applied(): lax.ppermute(part_b, 'rsec', shifted_x(steps[i]))  11.3 us
    ppermute x3, waiting for transfers between devices, applied(): lax.ppermute(part_a, 'rsec', shifted_z(steps[i]))  7.66 us
    unnamed x42, local copies, waits for them, and re-layouts  5.59 us
    ppermute x3, starting transfers between devices, applied(): lax.ppermute(part_a, 'rsec', shifted_z(steps[i]))  4.81 us
  transfers between devices with their start and end apart: 23, of which 6 were waited for; matrix products, arithmetic and copies ran while one was open for 0% of the time, Pallas kernels for 10%

profile of v1, /device:TPU:1, one launch (start us, length us, event | category | flops | bytes accessed | tf_op | source)
XLA Modules:
  0.0 124.2 jit_solution(14841734839709032058)
XLA Ops:
  0.0 2.5 %shard_map.64 = (bf16[16,4,8,128]{3,2,1,0:T(8,128)(2,1)}, bf16[18,4,8,128]{3,2,1,0:T(8,128)(2,1)}, bf16[2,4,256,128]{3,2,1,0:T(8,128)(2,1)}, bf16[2,4,256,128]{3,2,1,0:T(8,128)(2,1)}) custom-call(s32[4]{0:T(128)} %left_size.5, s32[4]{0:T(128)} %right_size.5, bf16[2,4,128,512]{3,2,1,0:T(8,128)(2,1)} %two_site.1, bf16[34,4,8,128]{3,2,1,0:T(8,128)(2,1)} %left_env.1), custom_call_target="tpu_custom_call" | custom-call | flops 1048576 | bytes 2097152 | tf_op jit(solution)/shard_map/pallas_call | solution.py:65
  2.6 4.5 %collective-permute-start = (bf16[2,4,256,128]{3,2,1,0:T(8,128)(2,1)}, bf16[2,4,256,128]{3,2,1,0:T(8,128)(2,1)S(1)}, u32[]{:S(2)}, u32[]{:S(2)}) collective-permute-start(bf16[2,4,256,128]{3,2,1,0:T(8,128)(2,1)} %get-tuple-element.11.up), channel_id=1, source_target_pairs={{0,1},{1,2},{2,3},{3,4},{4,5},{5,6},{6,7},{7,8},{8,9},{9,10},{10,1... | collective-permute-start | bytes 1572872 | tf_op jit(solution)/shard_map/ppermute | solution.py:289
  7.1 1.7 %collective-permute-start.17 = (bf16[16,4,8,128]{3,2,1,0:T(8,128)(2,1)}, bf16[16,4,8,128]{3,2,1,0:T(8,128)(2,1)S(1)}, u32[]{:S(2)}, u32[]{:S(2)}) collective-permute-start(bf16[16,4,8,128]{3,2,1,0:T(8,128)(2,1)} %get-tuple-element.16.own), channel_id=1, source_target_pairs={{0,1},{1,2},{2,3},{3,0},{4,5},{5,6},{6,7},{7,4},{8,9},{9,10},{10,1... | collective-permute-start | bytes 393224 | tf_op jit(solution)/shard_map/ppermute | solution.py:282
  8.8 1.1 collective-permute-start.18
  9.8 2.1 %collective-permute-start.19 = (bf16[16,4,8,128]{3,2,1,0:T(8,128)(2,1)}, bf16[16,4,8,128]{3,2,1,0:T(8,128)(2,1)S(1)}, u32[]{:S(2)}, u32[]{:S(2)}) collective-permute-start(bf16[16,4,8,128]{3,2,1,0:T(8,128)(2,1)} %get-tuple-element.16.own), channel_id=1, source_target_pairs={{0,2},{1,3},{2,0},{3,1},{4,6},{5,7},{6,4},{7,5},{8,10},{9,11},{10,... | collective-permute-start | bytes 393224 | tf_op jit(solution)/shard_map/ppermute | solution.py:282
  11.9 1.2 collective-permute-start.4
  13.1 7.7 %collective-permute-done.17.left = bf16[16,4,8,128]{3,2,1,0:T(8,128)(2,1)S(1)} collective-permute-done((bf16[16,4,8,128]{3,2,1,0:T(8,128)(2,1)}, bf16[16,4,8,128]{3,2,1,0:T(8,128)(2,1)S(1)}, u32[]{:S(2)}, u32[]{:S(2)}) %collective-permute-start.17) | collective-permute-done | bytes 131104 | tf_op jit(solution)/shard_map/ppermute | solution.py:282
  20.8 6.7 %collective-permute-start.5 = (bf16[18,4,8,128]{3,2,1,0:T(8,128)(2,1)}, bf16[18,4,8,128]{3,2,1,0:T(8,128)(2,1)S(1)}, u32[]{:S(2)}, u32[]{:S(2)}) collective-permute-start(bf16[18,4,8,128]{3,2,1,0:T(8,128)(2,1)} %get-tuple-element.15.own), channel_id=1, source_target_pairs={{0,12},{1,13},{2,14},{3,15},{4,0},{5,1},{6,2},{7,3},{8,4},{9,5},{1... | collective-permute-start | bytes 442376 | tf_op jit(solution)/shard_map/ppermute | solution.py:283
  27.4 1.3 %collective-permute-start.10 = (bf16[34,4,16,128]{3,2,1,0:T(8,128)(2,1)}, bf16[34,4,16,128]{3,2,1,0:T(8,128)(2,1)S(1)}, u32[]{:S(2)}, u32[]{:S(2)}) collective-permute-start(bf16[34,4,16,128]{3,2,1,0:T(8,128)(2,1)} %rights_0_.3), channel_id=1, source_target_pairs={{0,32},{16,48},{32,64},{48,80},{64,96},{80,112},{96,0},{112,16},{1... | collective-permute-start | bytes 1671176 | tf_op jit(solution)/shard_map/ppermute | solution.py:280
  28.7 1.5 %collective-permute-start.11 = (bf16[34,4,16,128]{3,2,1,0:T(8,128)(2,1)}, bf16[34,4,16,128]{3,2,1,0:T(8,128)(2,1)S(1)}, u32[]{:S(2)}, u32[]{:S(2)}) collective-permute-start(bf16[34,4,16,128]{3,2,1,0:T(8,128)(2,1)} %rights_0_.3), channel_id=1, source_target_pairs={{0,96},{16,112},{32,0},{48,16},{64,32},{80,48},{96,64},{112,80},{1... | collective-permute-start | bytes 1671176 | tf_op jit(solution)/shard_map/ppermute | solution.py:280
  30.3 1.3 %collective-permute-start.1 = (bf16[2,4,256,128]{3,2,1,0:T(8,128)(2,1)}, bf16[2,4,256,128]{3,2,1,0:T(8,128)(2,1)S(1)}, u32[]{:S(2)}, u32[]{:S(2)}) collective-permute-start(bf16[2,4,256,128]{3,2,1,0:T(8,128)(2,1)} %get-tuple-element.12.down), channel_id=1, source_target_pairs={{1,0},{2,1},{3,2},{4,3},{5,4},{6,5},{7,6},{8,7},{9,8},{10,9},{11,1... | collective-permute-start | bytes 1572872 | tf_op jit(solution)/shard_map/ppermute | solution.py:290
  31.6 3.4 %collective-permute-start.6 = (bf16[18,4,8,128]{3,2,1,0:T(8,128)(2,1)}, bf16[18,4,8,128]{3,2,1,0:T(8,128)(2,1)S(1)}, u32[]{:S(2)}, u32[]{:S(2)}) collective-permute-start(bf16[18,4,8,128]{3,2,1,0:T(8,128)(2,1)} %get-tuple-element.15.own), channel_id=1, source_target_pairs={{0,8},{1,9},{2,10},{3,11},{4,12},{5,13},{6,14},{7,15},{8,0},{9,1},... | collective-permute-start | bytes 442376 | tf_op jit(solution)/shard_map/ppermute | solution.py:283
  35.0 2.7 %collective-permute-done.6.far = bf16[18,4,8,128]{3,2,1,0:T(8,128)(2,1)S(1)} collective-permute-done((bf16[18,4,8,128]{3,2,1,0:T(8,128)(2,1)}, bf16[18,4,8,128]{3,2,1,0:T(8,128)(2,1)S(1)}, u32[]{:S(2)}, u32[]{:S(2)}) %collective-permute-start.6) | collective-permute-done | bytes 147488 | tf_op jit(solution)/shard_map/ppermute | solution.py:283
  37.7 1.2 %collective-permute-start.12 = (bf16[34,4,16,128]{3,2,1,0:T(8,128)(2,1)}, bf16[34,4,16,128]{3,2,1,0:T(8,128)(2,1)S(1)}, u32[]{:S(2)}, u32[]{:S(2)}) collective-permute-start(bf16[34,4,16,128]{3,2,1,0:T(8,128)(2,1)} %rights_0_.3), channel_id=1, source_target_pairs={{0,64},{16,80},{32,96},{48,112},{64,0},{80,16},{96,32},{112,48},{1... | collective-permute-start | bytes 1671176 | tf_op jit(solution)/shard_map/ppermute | solution.py:280
  39.0 3.0 %collective-permute-start.13 = (bf16[34,4,16,128]{3,2,1,0:T(8,128)(2,1)}, bf16[34,4,16,128]{3,2,1,0:T(8,128)(2,1)S(1)}, u32[]{:S(2)}, u32[]{:S(2)}) collective-permute-start(bf16[34,4,16,128]{3,2,1,0:T(8,128)(2,1)} %rights_0_.3), channel_id=1, source_target_pairs={{0,16},{16,0},{32,48},{48,32},{64,80},{80,64},{96,112},{112,96},{1... | collective-permute-start | bytes 1671176 | tf_op jit(solution)/shard_map/ppermute | solution.py:299
  42.0 0.9 copy-done.7
  43.0 1.0 collective-permute-done.1.high_r
  44.0 9.1 %collective-permute-start.20 = (bf16[4,16,4,8,128]{4,3,2,1,0:T(8,128)(2,1)S(1)}, bf16[4,16,4,8,128]{4,3,2,1,0:T(8,128)(2,1)S(1)}, u32[]{:S(2)}, u32[]{:S(2)}) collective-permute-start(bf16[4,16,4,8,128]{4,3,2,1,0:T(8,128)(2,1)S(1)} %shard_map.67.lefts_0_), channel_id=1, source_target_pairs={{0,4},{1,5},{2,6},{3,7},{4,8},{5,9},{6,10},{7,11},{8,12},{9,13},{1... | collective-permute-start | bytes 1572872 | tf_op jit(solution)/shard_map/ppermute | solution.py:293
  53.1 1.9 %collective-permute-start.21 = (bf16[4,16,4,8,128]{4,3,2,1,0:T(8,128)(2,1)S(1)}, bf16[4,16,4,8,128]{4,3,2,1,0:T(8,128)(2,1)S(1)}, u32[]{:S(2)}, u32[]{:S(2)}) collective-permute-start(bf16[4,16,4,8,128]{4,3,2,1,0:T(8,128)(2,1)S(1)} %shard_map.67.lefts_0_), channel_id=1, source_target_pairs={{0,12},{1,13},{2,14},{3,15},{4,0},{5,1},{6,2},{7,3},{8,4},{9,5},{1... | collective-permute-start | bytes 1572872 | tf_op jit(solution)/shard_map/ppermute | solution.py:293
  55.0 1.2 collective-permute-start.22
  56.2 1.0 copy-done.2
  57.2 1.0 copy-done.3
  58.4 2.9 %collective-permute-start.2 = (bf16[8,2,256,128]{3,2,1,0:T(8,128)(2,1)S(1)}, bf16[8,2,256,128]{3,2,1,0:T(8,128)(2,1)S(1)}, u32[]{:S(2)}, u32[]{:S(2)}) collective-permute-start(bf16[8,2,256,128]{3,2,1,0:T(8,128)(2,1)S(1)} %get-tuple-element.13), channel_id=1, source_target_pairs={{0,16},{16,32},{32,48},{48,64},{64,80},{80,96},{96,112},{1,17},{17... | collective-permute-start | bytes 3145736 | tf_op jit(solution)/shard_map/ppermute | solution.py:295
  61.4 2.5 %collective-permute-start.3 = (bf16[8,2,256,128]{3,2,1,0:T(8,128)(2,1)S(1)}, bf16[8,2,256,128]{3,2,1,0:T(8,128)(2,1)S(1)}, u32[]{:S(2)}, u32[]{:S(2)}) collective-permute-start(bf16[8,2,256,128]{3,2,1,0:T(8,128)(2,1)S(1)} %get-tuple-element.14), channel_id=1, source_target_pairs={{16,0},{32,16},{48,32},{64,48},{80,64},{96,80},{112,96},{17,1},{33... | collective-permute-start | bytes 3145736 | tf_op jit(solution)/shard_map/ppermute | solution.py:296
  63.9 3.1 %collective-permute-done.20.lefts_1_ = bf16[4,16,4,8,128]{4,3,2,1,0:T(8,128)(2,1)S(1)} collective-permute-done((bf16[4,16,4,8,128]{4,3,2,1,0:T(8,128)(2,1)S(1)}, bf16[4,16,4,8,128]{4,3,2,1,0:T(8,128)(2,1)S(1)}, u32[]{:S(2)}, u32[]{:S(2)}) %collective-permute-start.20) | collective-permute-done | bytes 524320 | tf_op jit(solution)/shard_map/ppermute | solution.py:293
  67.8 10.6 %collective-permute-start.15 = (bf16[34,4,16,128]{3,2,1,0:T(8,128)(2,1)S(1)}, bf16[34,4,16,128]{3,2,1,0:T(8,128)(2,1)S(1)}, u32[]{:S(2)}, u32[]{:S(2)}) collective-permute-start(bf16[34,4,16,128]{3,2,1,0:T(8,128)(2,1)S(1)} %collective-permute-done.11.rights_2_), channel_id=1, source_target_pairs={{0,16},{16,0},{32,48},{48,32},{64,80},{80,64},{96,112},{112,96},{1... | collective-permute-start | bytes 1671176 | tf_op jit(solution)/shard_map/ppermute | solution.py:299
  79.2 1.0 collective-permute-start.16
  80.4 2.6 %collective-permute-start.8 = (bf16[4,18,4,8,128]{4,3,2,1,0:T(8,128)(2,1)S(1)}, bf16[4,18,4,8,128]{4,3,2,1,0:T(8,128)(2,1)}, u32[]{:S(2)}, u32[]{:S(2)}) collective-permute-start(bf16[4,18,4,8,128]{4,3,2,1,0:T(8,128)(2,1)S(1)} %shard_map.66.lefts_0_), channel_id=1, source_target_pairs={{0,3},{1,0},{2,1},{3,2},{4,7},{5,4},{6,5},{7,6},{8,11},{9,8},{10,9... | collective-permute-start | bytes 1769480 | tf_op jit(solution)/shard_map/ppermute | solution.py:302
  83.8 1.0 copy-done.9
  84.9 12.8 %shard_map.68.rest_0_ = f32[4,4,128,256]{3,2,1,0:T(8,128)} custom-call(s32[2,34]{1,0:T(2,128)} %bitcast.1, s32[4]{0:T(128)} %left_size.5, s32[4]{0:T(128)} %right_size.5, bf16[2,4,256,128]{3,2,1,0:T(8,128)(2,1)} %copy-done.4, bf16[2,4,256,128]{3,2,1,0:T(8,128)(2,1)} %get-tuple-element.12.down, bf16[2,4,256,128]{3,2,1,0:T(8,128)(2,1)} %get-tuple-element.11.up, ...), custom_call_target="tpu_custom_call" | custom-call | flops 4294967296 | bytes 10485760 | tf_op jit(solution)/shard_map/pallas_call | solution.py:265
  97.7 11.4 %collective-permute-done.7.lefts_1_ = bf16[4,18,4,8,128]{4,3,2,1,0:T(8,128)(2,1)S(1)} collective-permute-done((bf16[4,18,4,8,128]{4,3,2,1,0:T(8,128)(2,1)S(1)}, bf16[4,18,4,8,128]{4,3,2,1,0:T(8,128)(2,1)S(1)}, u32[]{:S(2)}, u32[]{:S(2)}) %collective-permute-start.7) | collective-permute-done | bytes 589856 | tf_op jit(solution)/shard_map/ppermute | solution.py:302
  109.9 14.2 %shard_map.69 = bf16[2,4,128,512]{3,2,1,0:T(8,128)(2,1)} custom-call(s32[2,34]{1,0:T(2,128)} %bitcast.2, s32[4]{0:T(128)} %left_size.5, s32[4]{0:T(128)} %right_size.5, bf16[2,4,256,128]{3,2,1,0:T(8,128)(2,1)} %copy-done.4, bf16[2,4,256,128]{3,2,1,0:T(8,128)(2,1)} %get-tuple-element.12.down, bf16[2,4,256,128]{3,2,1,0:T(8,128)(2,1)} %get-tuple-element.11.up, ...), custom_call_target="tpu_custom_call" | custom-call | flops 4831838208 | bytes 10485760 | tf_op jit(solution)/shard_map/pallas_call | solution.py:265
  (62 shorter events, 3.4 us)
Async XLA Ops:
  2.5 77.6 %copy-start.6 = (bf16[18,4,8,128]{3,2,1,0:T(8,128)(2,1)S(1)}, bf16[18,4,8,128]{3,2,1,0:T(8,128)(2,1)}, u32[]{:S(2)}) copy-start(bf16[18,4,8,128]{3,2,1,0:T(8,128)(2,1)} %get-tuple-element.15.own) | copy-start | bytes 442372
  2.6 36.4 %collective-permute-start = (bf16[2,4,256,128]{3,2,1,0:T(8,128)(2,1)}, bf16[2,4,256,128]{3,2,1,0:T(8,128)(2,1)S(1)}, u32[]{:S(2)}, u32[]{:S(2)}) collective-permute-start(bf16[2,4,256,128]{3,2,1,0:T(8,128)(2,1)} %get-tuple-element.11.up), channel_id=1, source_target_pairs={{0,1},{1,2},{2,3},{3,4},{4,5},{5,6},{6,7},{7,8},{8,9},{9,10},{10,1... | collective-permute-start | bytes 1572872 | tf_op jit(solution)/shard_map/ppermute | solution.py:289
  7.1 13.7 %collective-permute-start.17 = (bf16[16,4,8,128]{3,2,1,0:T(8,128)(2,1)}, bf16[16,4,8,128]{3,2,1,0:T(8,128)(2,1)S(1)}, u32[]{:S(2)}, u32[]{:S(2)}) collective-permute-start(bf16[16,4,8,128]{3,2,1,0:T(8,128)(2,1)} %get-tuple-element.16.own), channel_id=1, source_target_pairs={{0,1},{1,2},{2,3},{3,0},{4,5},{5,6},{6,7},{7,4},{8,9},{9,10},{10,1... | collective-permute-start | bytes 393224 | tf_op jit(solution)/shard_map/ppermute | solution.py:282
  8.8 18.7 %collective-permute-start.18 = (bf16[16,4,8,128]{3,2,1,0:T(8,128)(2,1)}, bf16[16,4,8,128]{3,2,1,0:T(8,128)(2,1)S(1)}, u32[]{:S(2)}, u32[]{:S(2)}) collective-permute-start(bf16[16,4,8,128]{3,2,1,0:T(8,128)(2,1)} %get-tuple-element.16.own), channel_id=1, source_target_pairs={{0,3},{1,0},{2,1},{3,2},{4,7},{5,4},{6,5},{7,6},{8,11},{9,8},{10,9... | collective-permute-start | bytes 393224 | tf_op jit(solution)/shard_map/ppermute | solution.py:282
  9.8 18.9 %collective-permute-start.19 = (bf16[16,4,8,128]{3,2,1,0:T(8,128)(2,1)}, bf16[16,4,8,128]{3,2,1,0:T(8,128)(2,1)S(1)}, u32[]{:S(2)}, u32[]{:S(2)}) collective-permute-start(bf16[16,4,8,128]{3,2,1,0:T(8,128)(2,1)} %get-tuple-element.16.own), channel_id=1, source_target_pairs={{0,2},{1,3},{2,0},{3,1},{4,6},{5,7},{6,4},{7,5},{8,10},{9,11},{10,... | collective-permute-start | bytes 393224 | tf_op jit(solution)/shard_map/ppermute | solution.py:282
  11.9 18.4 %collective-permute-start.4 = (bf16[18,4,8,128]{3,2,1,0:T(8,128)(2,1)}, bf16[18,4,8,128]{3,2,1,0:T(8,128)(2,1)S(1)}, u32[]{:S(2)}, u32[]{:S(2)}) collective-permute-start(bf16[18,4,8,128]{3,2,1,0:T(8,128)(2,1)} %get-tuple-element.15.own), channel_id=1, source_target_pairs={{0,4},{1,5},{2,6},{3,7},{4,8},{5,9},{6,10},{7,11},{8,12},{9,13},{1... | collective-permute-start | bytes 442376 | tf_op jit(solution)/shard_map/ppermute | solution.py:283
  20.8 10.8 %collective-permute-start.5 = (bf16[18,4,8,128]{3,2,1,0:T(8,128)(2,1)}, bf16[18,4,8,128]{3,2,1,0:T(8,128)(2,1)S(1)}, u32[]{:S(2)}, u32[]{:S(2)}) collective-permute-start(bf16[18,4,8,128]{3,2,1,0:T(8,128)(2,1)} %get-tuple-element.15.own), channel_id=1, source_target_pairs={{0,12},{1,13},{2,14},{3,15},{4,0},{5,1},{6,2},{7,3},{8,4},{9,5},{1... | collective-permute-start | bytes 442376 | tf_op jit(solution)/shard_map/ppermute | solution.py:283
  27.4 25.7 %collective-permute-start.10 = (bf16[34,4,16,128]{3,2,1,0:T(8,128)(2,1)}, bf16[34,4,16,128]{3,2,1,0:T(8,128)(2,1)S(1)}, u32[]{:S(2)}, u32[]{:S(2)}) collective-permute-start(bf16[34,4,16,128]{3,2,1,0:T(8,128)(2,1)} %rights_0_.3), channel_id=1, source_target_pairs={{0,32},{16,48},{32,64},{48,80},{64,96},{80,112},{96,0},{112,16},{1... | collective-permute-start | bytes 1671176 | tf_op jit(solution)/shard_map/ppermute | solution.py:280
  28.7 26.3 %collective-permute-start.11 = (bf16[34,4,16,128]{3,2,1,0:T(8,128)(2,1)}, bf16[34,4,16,128]{3,2,1,0:T(8,128)(2,1)S(1)}, u32[]{:S(2)}, u32[]{:S(2)}) collective-permute-start(bf16[34,4,16,128]{3,2,1,0:T(8,128)(2,1)} %rights_0_.3), channel_id=1, source_target_pairs={{0,96},{16,112},{32,0},{48,16},{64,32},{80,48},{96,64},{112,80},{1... | collective-permute-start | bytes 1671176 | tf_op jit(solution)/shard_map/ppermute | solution.py:280
  30.3 13.8 %collective-permute-start.1 = (bf16[2,4,256,128]{3,2,1,0:T(8,128)(2,1)}, bf16[2,4,256,128]{3,2,1,0:T(8,128)(2,1)S(1)}, u32[]{:S(2)}, u32[]{:S(2)}) collective-permute-start(bf16[2,4,256,128]{3,2,1,0:T(8,128)(2,1)} %get-tuple-element.12.down), channel_id=1, source_target_pairs={{1,0},{2,1},{3,2},{4,3},{5,4},{6,5},{7,6},{8,7},{9,8},{10,9},{11,1... | collective-permute-start | bytes 1572872 | tf_op jit(solution)/shard_map/ppermute | solution.py:290
  31.6 6.2 %collective-permute-start.6 = (bf16[18,4,8,128]{3,2,1,0:T(8,128)(2,1)}, bf16[18,4,8,128]{3,2,1,0:T(8,128)(2,1)S(1)}, u32[]{:S(2)}, u32[]{:S(2)}) collective-permute-start(bf16[18,4,8,128]{3,2,1,0:T(8,128)(2,1)} %get-tuple-element.15.own), channel_id=1, source_target_pairs={{0,8},{1,9},{2,10},{3,11},{4,12},{5,13},{6,14},{7,15},{8,0},{9,1},... | collective-permute-start | bytes 442376 | tf_op jit(solution)/shard_map/ppermute | solution.py:283
  37.7 20.7 %collective-permute-start.12 = (bf16[34,4,16,128]{3,2,1,0:T(8,128)(2,1)}, bf16[34,4,16,128]{3,2,1,0:T(8,128)(2,1)S(1)}, u32[]{:S(2)}, u32[]{:S(2)}) collective-permute-start(bf16[34,4,16,128]{3,2,1,0:T(8,128)(2,1)} %rights_0_.3), channel_id=1, source_target_pairs={{0,64},{16,80},{32,96},{48,112},{64,0},{80,16},{96,32},{112,48},{1... | collective-permute-start | bytes 1671176 | tf_op jit(solution)/shard_map/ppermute | solution.py:280
  39.0 41.2 %copy-start.4 = (bf16[2,4,256,128]{3,2,1,0:T(8,128)(2,1)}, bf16[2,4,256,128]{3,2,1,0:T(8,128)(2,1)S(1)}, u32[]{:S(2)}) copy-start(bf16[2,4,256,128]{3,2,1,0:T(8,128)(2,1)S(1)} %collective-permute-done.low_r) | copy-start | bytes 1572868
  39.0 22.3 %collective-permute-start.13 = (bf16[34,4,16,128]{3,2,1,0:T(8,128)(2,1)}, bf16[34,4,16,128]{3,2,1,0:T(8,128)(2,1)S(1)}, u32[]{:S(2)}, u32[]{:S(2)}) collective-permute-start(bf16[34,4,16,128]{3,2,1,0:T(8,128)(2,1)} %rights_0_.3), channel_id=1, source_target_pairs={{0,16},{16,0},{32,48},{48,32},{64,80},{80,64},{96,112},{112,96},{1... | collective-permute-start | bytes 1671176 | tf_op jit(solution)/shard_map/ppermute | solution.py:299
  43.0 41.9 %copy-start.1 = (bf16[4,16,4,8,128]{4,3,2,1,0:T(8,128)(2,1)}, bf16[4,16,4,8,128]{4,3,2,1,0:T(8,128)(2,1)S(1)}, u32[]{:S(2)}) copy-start(bf16[4,16,4,8,128]{4,3,2,1,0:T(8,128)(2,1)S(1)} %shard_map.67.lefts_0_) | copy-start | bytes 1572868
  44.0 40.9 %copy-start.5 = (bf16[2,4,256,128]{3,2,1,0:T(8,128)(2,1)}, bf16[2,4,256,128]{3,2,1,0:T(8,128)(2,1)S(1)}, u32[]{:S(2)}) copy-start(bf16[2,4,256,128]{3,2,1,0:T(8,128)(2,1)S(1)} %collective-permute-done.1.high_r) | copy-start | bytes 1572868
  44.0 23.0 %collective-permute-start.20 = (bf16[4,16,4,8,128]{4,3,2,1,0:T(8,128)(2,1)S(1)}, bf16[4,16,4,8,128]{4,3,2,1,0:T(8,128)(2,1)S(1)}, u32[]{:S(2)}, u32[]{:S(2)}) collective-permute-start(bf16[4,16,4,8,128]{4,3,2,1,0:T(8,128)(2,1)S(1)} %shard_map.67.lefts_0_), channel_id=1, source_target_pairs={{0,4},{1,5},{2,6},{3,7},{4,8},{5,9},{6,10},{7,11},{8,12},{9,13},{1... | collective-permute-start | bytes 1572872 | tf_op jit(solution)/shard_map/ppermute | solution.py:293
  53.1 29.9 %copy-start.11 = (bf16[34,4,16,128]{3,2,1,0:T(8,128)(2,1)}, bf16[34,4,16,128]{3,2,1,0:T(8,128)(2,1)S(1)}, u32[]{:S(2)}) copy-start(bf16[34,4,16,128]{3,2,1,0:T(8,128)(2,1)S(1)} %collective-permute-done.10.rights_1_) | copy-start | bytes 1671172
  53.1 14.6 %collective-permute-start.21 = (bf16[4,16,4,8,128]{4,3,2,1,0:T(8,128)(2,1)S(1)}, bf16[4,16,4,8,128]{4,3,2,1,0:T(8,128)(2,1)S(1)}, u32[]{:S(2)}, u32[]{:S(2)}) collective-permute-start(bf16[4,16,4,8,128]{4,3,2,1,0:T(8,128)(2,1)S(1)} %shard_map.67.lefts_0_), channel_id=1, source_target_pairs={{0,12},{1,13},{2,14},{3,15},{4,0},{5,1},{6,2},{7,3},{8,4},{9,5},{1... | collective-permute-start | bytes 1572872 | tf_op jit(solution)/shard_map/ppermute | solution.py:293
  55.0 28.1 %copy-start.12 = (bf16[34,4,16,128]{3,2,1,0:T(8,128)(2,1)}, bf16[34,4,16,128]{3,2,1,0:T(8,128)(2,1)S(1)}, u32[]{:S(2)}) copy-start(bf16[34,4,16,128]{3,2,1,0:T(8,128)(2,1)S(1)} %collective-permute-done.11.rights_2_) | copy-start | bytes 1671172
  55.0 24.2 %collective-permute-start.22 = (bf16[4,16,4,8,128]{4,3,2,1,0:T(8,128)(2,1)S(1)}, bf16[4,16,4,8,128]{4,3,2,1,0:T(8,128)(2,1)S(1)}, u32[]{:S(2)}, u32[]{:S(2)}) collective-permute-start(bf16[4,16,4,8,128]{4,3,2,1,0:T(8,128)(2,1)S(1)} %shard_map.67.lefts_0_), channel_id=1, source_target_pairs={{0,8},{1,9},{2,10},{3,11},{4,12},{5,13},{6,14},{7,15},{8,0},{9,1},... | collective-permute-start | bytes 1572872 | tf_op jit(solution)/shard_map/ppermute | solution.py:293
  58.4 24.7 %copy-start.13 = (bf16[34,4,16,128]{3,2,1,0:T(8,128)(2,1)}, bf16[34,4,16,128]{3,2,1,0:T(8,128)(2,1)S(1)}, u32[]{:S(2)}) copy-start(bf16[34,4,16,128]{3,2,1,0:T(8,128)(2,1)S(1)} %collective-permute-done.12.rights_3_) | copy-start | bytes 1671172
  58.4 24.6 %collective-permute-start.2 = (bf16[8,2,256,128]{3,2,1,0:T(8,128)(2,1)S(1)}, bf16[8,2,256,128]{3,2,1,0:T(8,128)(2,1)S(1)}, u32[]{:S(2)}, u32[]{:S(2)}) collective-permute-start(bf16[8,2,256,128]{3,2,1,0:T(8,128)(2,1)S(1)} %get-tuple-element.13), channel_id=1, source_target_pairs={{0,16},{16,32},{32,48},{48,64},{64,80},{80,96},{96,112},{1,17},{17... | collective-permute-start | bytes 3145736 | tf_op jit(solution)/shard_map/ppermute | solution.py:295
  61.3 21.7 %copy-start.14 = (bf16[34,4,16,128]{3,2,1,0:T(8,128)(2,1)}, bf16[34,4,16,128]{3,2,1,0:T(8,128)(2,1)S(1)}, u32[]{:S(2)}) copy-start(bf16[34,4,16,128]{3,2,1,0:T(8,128)(2,1)S(1)} %collective-permute-done.13.partners_0_) | copy-start | bytes 1671172
  61.4 21.7 %collective-permute-start.3 = (bf16[8,2,256,128]{3,2,1,0:T(8,128)(2,1)S(1)}, bf16[8,2,256,128]{3,2,1,0:T(8,128)(2,1)S(1)}, u32[]{:S(2)}, u32[]{:S(2)}) collective-permute-start(bf16[8,2,256,128]{3,2,1,0:T(8,128)(2,1)S(1)} %get-tuple-element.14), channel_id=1, source_target_pairs={{16,0},{32,16},{48,32},{64,48},{80,64},{96,80},{112,96},{17,1},{33... | collective-permute-start | bytes 3145736 | tf_op jit(solution)/shard_map/ppermute | solution.py:296
  67.0 13.2 %collective-permute-start.14 = (bf16[34,4,16,128]{3,2,1,0:T(8,128)(2,1)S(1)}, bf16[34,4,16,128]{3,2,1,0:T(8,128)(2,1)S(1)}, u32[]{:S(2)}, u32[]{:S(2)}) collective-permute-start(bf16[34,4,16,128]{3,2,1,0:T(8,128)(2,1)S(1)} %collective-permute-done.10.rights_1_), channel_id=1, source_target_pairs={{0,16},{16,0},{32,48},{48,32},{64,80},{80,64},{96,112},{112,96},{1... | collective-permute-start | bytes 1671176 | tf_op jit(solution)/shard_map/ppermute | solution.py:299
  67.8 12.6 %collective-permute-start.15 = (bf16[34,4,16,128]{3,2,1,0:T(8,128)(2,1)S(1)}, bf16[34,4,16,128]{3,2,1,0:T(8,128)(2,1)S(1)}, u32[]{:S(2)}, u32[]{:S(2)}) collective-permute-start(bf16[34,4,16,128]{3,2,1,0:T(8,128)(2,1)S(1)} %collective-permute-done.11.rights_2_), channel_id=1, source_target_pairs={{0,16},{16,0},{32,48},{48,32},{64,80},{80,64},{96,112},{112,96},{1... | collective-permute-start | bytes 1671176 | tf_op jit(solution)/shard_map/ppermute | solution.py:299
  79.2 3.9 %collective-permute-start.16 = (bf16[34,4,16,128]{3,2,1,0:T(8,128)(2,1)S(1)}, bf16[34,4,16,128]{3,2,1,0:T(8,128)(2,1)S(1)}, u32[]{:S(2)}, u32[]{:S(2)}) collective-permute-start(bf16[34,4,16,128]{3,2,1,0:T(8,128)(2,1)S(1)} %collective-permute-done.12.rights_3_), channel_id=1, source_target_pairs={{0,16},{16,0},{32,48},{48,32},{64,80},{80,64},{96,112},{112,96},{1... | collective-permute-start | bytes 1671176 | tf_op jit(solution)/shard_map/ppermute | solution.py:299
  80.2 17.4 %copy-start = (bf16[4,18,4,8,128]{4,3,2,1,0:T(8,128)(2,1)}, bf16[4,18,4,8,128]{4,3,2,1,0:T(8,128)(2,1)S(1)}, u32[]{:S(2)}) copy-start(bf16[4,18,4,8,128]{4,3,2,1,0:T(8,128)(2,1)S(1)} %shard_map.66.lefts_0_) | copy-start | bytes 1769476
  80.3 28.8 %collective-permute-start.7 = (bf16[4,18,4,8,128]{4,3,2,1,0:T(8,128)(2,1)S(1)}, bf16[4,18,4,8,128]{4,3,2,1,0:T(8,128)(2,1)S(1)}, u32[]{:S(2)}, u32[]{:S(2)}) collective-permute-start(bf16[4,18,4,8,128]{4,3,2,1,0:T(8,128)(2,1)S(1)} %shard_map.66.lefts_0_), channel_id=1, source_target_pairs={{0,1},{1,2},{2,3},{3,0},{4,5},{5,6},{6,7},{7,4},{8,9},{9,10},{10,1... | collective-permute-start | bytes 1769480 | tf_op jit(solution)/shard_map/ppermute | solution.py:302
  80.4 28.7 %collective-permute-start.8 = (bf16[4,18,4,8,128]{4,3,2,1,0:T(8,128)(2,1)S(1)}, bf16[4,18,4,8,128]{4,3,2,1,0:T(8,128)(2,1)}, u32[]{:S(2)}, u32[]{:S(2)}) collective-permute-start(bf16[4,18,4,8,128]{4,3,2,1,0:T(8,128)(2,1)S(1)} %shard_map.66.lefts_0_), channel_id=1, source_target_pairs={{0,3},{1,0},{2,1},{3,2},{4,7},{5,4},{6,5},{7,6},{8,11},{9,8},{10,9... | collective-permute-start | bytes 1769480 | tf_op jit(solution)/shard_map/ppermute | solution.py:302
  83.0 26.0 %collective-permute-start.9 = (bf16[4,18,4,8,128]{4,3,2,1,0:T(8,128)(2,1)S(1)}, bf16[4,18,4,8,128]{4,3,2,1,0:T(8,128)(2,1)}, u32[]{:S(2)}, u32[]{:S(2)}) collective-permute-start(bf16[4,18,4,8,128]{4,3,2,1,0:T(8,128)(2,1)S(1)} %shard_map.66.lefts_0_), channel_id=1, source_target_pairs={{0,2},{1,3},{2,0},{3,1},{4,6},{5,7},{6,4},{7,5},{8,10},{9,11},{10,... | collective-permute-start | bytes 1769480 | tf_op jit(solution)/shard_map/ppermute | solution.py:302
  (12 other events, 48.5 us)
